TPU v7x, 128 devices: a whole 4x4x4 slice. The times are simulated.
128 devices in a mesh: gossip: 4 (over x_hi, core), field: 32 (over x_lo, z, y).
Axes of the slice: x: 4 (x_hi: 2, x_lo: 2; x = x_hi * 2 + x_lo), y: 4, z: 4, core: 2. Of those that a mesh axis runs over, the one named last changes fastest.
Arguments:
- measured_features: bfloat16 [8, 128, 96, 512], P('gossip', 'field'), may hold values from -6 to 6
- feeder_of_row: int32 [128], P('field'), may hold values from 0 to 127, each once
- feeder_table: bfloat16 [128, 512], replicated, may hold values from -3 to 3
- time_qkv: bfloat16 [512, 1536], replicated, may hold values from -0.25 to 0.25
- time_out: bfloat16 [512, 512], replicated, may hold values from -0.25 to 0.25
- feed_qkv: bfloat16 [512, 1536], replicated, may hold values from -0.25 to 0.25
- feed_out: bfloat16 [512, 512], replicated, may hold values from -0.25 to 0.25
- adjoint_of_prediction: bfloat16 [8, 128, 96, 512], P('gossip', None, 'field'), may hold values from -0.09375 to 0.09375
- round_index: int32 [1], replicated, may hold values from 0 to 1
Outputs:
- predicted_load: bfloat16 [8, 128, 96, 512], P('gossip', None, 'field')
- peer_mean_derivatives: float32 [4, 4096, 512], P('gossip')
All inputs are finite; a program needn't handle non-finite values.
Results may differ from a plain program's by a relative error of at most 0.02.
Values may be sent and summed in bfloat16 or wider, within the bound.
A program may use at most 128 MiB of HBM per device.

v0:
```python
from functools import partial
import math

import jax
import jax.numpy as jnp
import numpy as np
from jax import lax
from jax.experimental import pallas as pl
from jax.experimental.pallas import tpu as pltpu
from jax.sharding import PartitionSpec as P

epsilon = 1e-05


MESH = pl.DeviceIdType.MESH
LANES = 128
LINKS = ("ya", "za", "xa", "yb", "zb")
PAIRS = ("core", "xb")
GROUPS = (1, 2, 2)
STEPS = len(GROUPS)
TURNS = 2 * STEPS + 1
COPIES = sum(2**size - 1 for size in GROUPS)


class Place:
    def __init__(self):
        gossip, field = lax.axis_index("gossip"), lax.axis_index("field")
        x_hi, core = gossip // 2, gossip % 2
        x_lo, z, y = field // 16, (field // 4) % 4, field % 4
        self.here = {"x_hi": x_hi, "core": core, "x_lo": x_lo, "z": z, "y": y}
        self.bit = {
            "ya": ((y + 1) // 2) % 2,
            "yb": y // 2,
            "za": ((z + 1) // 2) % 2,
            "zb": z // 2,
            "xa": (x_hi + x_lo) % 2,
        }
        self.flip = {
            "ya": {"y": y + 1 - 2 * (y % 2)},
            "yb": {"y": 3 - y},
            "za": {"z": z + 1 - 2 * (z % 2)},
            "zb": {"z": 3 - z},
            "xa": {"x_lo": 1 - x_lo},
            "xb": {"x_hi": 1 - x_hi, "x_lo": 1 - x_lo},
            "core": {"core": 1 - core},
        }

    def across(self, *names):
        at = dict(self.here)
        for name in names:
            at.update(self.flip[name])
        return (at["x_hi"] * 2 + at["core"], (at["x_lo"] * 4 + at["z"]) * 4 + at["y"])


def chains_of(rows):
    unit = 512
    count, more = divmod(rows // unit, len(LINKS))
    chains, first = [], 0
    for turn in range(len(LINKS)):
        names = [LINKS[(turn + s) % len(LINKS)] for s in range(len(LINKS))]
        groups = tuple(tuple(names[sum(GROUPS[:s]) : sum(GROUPS[: s + 1])]) for s in range(STEPS))
        size = (count + (turn < more)) * unit
        chains.append((first, size, groups))
        first += size
    assert first == rows
    return chains


def block_of(rows):
    for parts in range(1, rows + 1):
        if rows % parts == 0 and rows // parts <= 256 and (rows // parts) % 16 == 0:
            return rows // parts
    return rows


class Reduction:
    def __init__(self, place, partner, g, inbox, pairbox, full, out, sems):
        self.place, self.partner = place, partner
        self.g, self.inbox, self.pairbox, self.full, self.out = g, inbox, pairbox, full, out
        self.rs_send, self.rs_recv, self.pair_send, self.pair_recv, self.ag_send, self.ag_recv, self.out_sem = sems
        self.chains = chains_of(g.shape[0])
        self.at = []
        self.steps = []
        for first, rows, groups in self.chains:
            at, size, sem, steps = [first], rows, 0, []
            for names in groups:
                part = size >> len(names)
                peers = []
                for mask in range(1, 2 ** len(names)):
                    flipped = [name for n, name in enumerate(names) if mask >> n & 1]
                    offset = at[-1]
                    for n, name in enumerate(names):
                        bit = place.bit[name]
                        offset = offset + (1 - bit if name in flipped else bit) * (size >> (n + 1))
                    slot = first + rows - size + (mask - 1) * part
                    peers.append((place.across(*flipped), offset, slot, sem))
                    sem += 1
                mine = at[-1]
                for n, name in enumerate(names):
                    mine = mine + place.bit[name] * (size >> (n + 1))
                steps.append((part, peers))
                at.append(mine)
                size = part
            self.at.append(at)
            self.steps.append(steps)

    def rs_copies(self, j, s):
        part, peers = self.steps[j][s]
        return [
            pltpu.make_async_remote_copy(
                src_ref=self.g.at[pl.ds(pl.multiple_of(offset, 16), part)],
                dst_ref=self.inbox.at[pl.ds(slot, part)],
                send_sem=self.rs_send.at[j, sem],
                recv_sem=self.rs_recv.at[j, sem],
                device_id=peer,
                device_id_type=MESH,
            )
            for peer, offset, slot, sem in peers
        ]

    def rs_add(self, j, s):
        part, peers = self.steps[j][s]
        keep = self.at[j][s + 1]
        block = block_of(part)

        def add(i, carry):
            here = pl.ds(pl.multiple_of(keep + i * block, 16), block)
            total = self.g[here, :].astype(jnp.float32)
            for peer, offset, slot, sem in peers:
                there = pl.ds(pl.multiple_of(slot + i * block, 16), block)
                total = total + self.inbox[there, :].astype(jnp.float32)
            self.g[here, :] = total.astype(jnp.bfloat16)
            return carry

        lax.fori_loop(0, part // block, add, 0)

    def shard(self, j):
        first, rows, groups = self.chains[j]
        count = rows >> len(LINKS)
        return pl.ds(pl.multiple_of(self.at[j][STEPS], 16), count), pl.ds(first >> len(LINKS), count)

    def pair_copy(self, j, n):
        here, there = self.shard(j)
        return pltpu.make_async_remote_copy(
            src_ref=self.g.at[here],
            dst_ref=self.pairbox.at[n, there],
            send_sem=self.pair_send.at[j, n],
            recv_sem=self.pair_recv.at[j, n],
            device_id=self.place.across(PAIRS[n]),
            device_id_type=MESH,
        )

    def pair_mean(self, j):
        here, there = self.shard(j)
        other = jnp.where(
            self.partner[0:1, :] > 0.0,
            self.pairbox[1, there, :].astype(jnp.float32),
            self.pairbox[0, there, :].astype(jnp.float32),
        )
        self.full[here, :] = ((self.g[here, :].astype(jnp.float32) + other) * 0.5).astype(jnp.bfloat16)

    def ag_copies(self, j, s):
        part, peers = self.steps[j][s]
        mine = self.full.at[pl.ds(pl.multiple_of(self.at[j][s + 1], 16), part)]
        return [
            pltpu.make_async_remote_copy(
                src_ref=mine,
                dst_ref=mine,
                send_sem=self.ag_send.at[j, sem],
                recv_sem=self.ag_recv.at[j, sem],
                device_id=peer,
                device_id_type=MESH,
            )
            for peer, offset, slot, sem in peers
        ]

    def out_copy(self, j):
        part = pl.ds(self.chains[j][0], self.chains[j][1])
        return pltpu.make_async_copy(self.full.at[part], self.out.at[part], self.out_sem.at[j])

    def start(self, begin, end):
        for j, (first, rows, groups) in enumerate(self.chains):
            if begin < first + rows <= end:
                for copy in self.rs_copies(j, 0):
                    copy.start()

    def turn(self, t, chains=None):
        if 0 <= t < TURNS:
            for j in range(len(self.chains)) if chains is None else chains:
                self.advance(j, t)

    def advance(self, j, stage):
        following = []
        if stage < STEPS:
            for copy in self.rs_copies(j, stage):
                copy.wait()
            self.rs_add(j, stage)
            if stage + 1 < STEPS:
                following = self.rs_copies(j, stage + 1)
            else:
                following = [self.pair_copy(j, n) for n in range(len(PAIRS))]
        elif stage == STEPS:
            for n in range(len(PAIRS)):
                self.pair_copy(j, n).wait()
            self.pair_mean(j)
            following = self.ag_copies(j, STEPS - 1)
        else:
            s = 2 * STEPS - stage
            for copy in self.ag_copies(j, s):
                copy.wait()
            following = self.ag_copies(j, s - 1) if s > 0 else [self.out_copy(j)]
        for copy in following:
            copy.start()

    def finish(self):
        for j in range(len(self.chains)):
            self.out_copy(j).wait()


class Exchange:
    def __init__(self, count, send, got, send_sem, recv_sem, own_sem):
        self.count, self.send, self.got = count, send, got
        self.send_sem, self.recv_sem, self.own_sem = send_sem, recv_sem, own_sem
        self.gossip, self.me = lax.axis_index("gossip"), lax.axis_index("field")
        self.rows = send.shape[0] // count

    def block(self, i):
        return pl.ds(pl.multiple_of(i * self.rows, 8), self.rows)

    def own(self):
        here = self.block(self.me)
        return pltpu.make_async_copy(self.send.at[here], self.got.at[here], self.own_sem)

    def copy(self, i):
        to = lax.rem(self.me + i, self.count)
        return pltpu.make_async_remote_copy(
            src_ref=self.send.at[self.block(to)],
            dst_ref=self.got.at[self.block(self.me)],
            send_sem=self.send_sem.at[i],
            recv_sem=self.recv_sem.at[i],
            device_id=(self.gossip, to),
            device_id_type=MESH,
        )

    def start(self):
        def one(i, carry):
            self.copy(i).start()
            return carry

        lax.fori_loop(1, self.count, one, 0)
        self.own().start()

    def wait(self):
        def one(i, carry):
            self.copy(i).wait()
            return carry

        lax.fori_loop(1, self.count, one, 0)
        self.own().wait()


def greet(place, count):
    barrier = pltpu.get_barrier_semaphore()
    gossip, me = lax.axis_index("gossip"), lax.axis_index("field")

    def one(i, carry):
        peer = (gossip, lax.rem(me + i, count))
        pl.semaphore_signal(barrier, inc=1, device_id=peer, device_id_type=MESH)
        return carry

    lax.fori_loop(1, count, one, 0)
    for name in PAIRS:
        pl.semaphore_signal(barrier, inc=1, device_id=place.across(name), device_id_type=MESH)


def all_greeted(count):
    pl.semaphore_wait(pltpu.get_barrier_semaphore(), count - 1 + len(PAIRS))


SIZE = 64
PAIR = 2 * SIZE


def dot(a, b, contract=((1,), (0,))):
    return lax.dot_general(a, b, (contract, ((), ())), preferred_element_type=jnp.float32)


NT = ((1,), (1,))
TN = ((0,), (0,))


def first_lanes(rows):
    return lax.broadcasted_iota(jnp.int32, (rows, PAIR), 1) < SIZE


def stacked(pair):
    low = first_lanes(pair.shape[0])
    nothing = jnp.zeros_like(pair)
    return jnp.concatenate([jnp.where(low, pair, nothing), jnp.where(low, nothing, pair)], axis=0)


def unstacked(both):
    rows = both.shape[0] // 2
    return jnp.where(first_lanes(rows), both[:rows], both[rows:])


def norm_factor(wide):
    return lax.rsqrt(jnp.mean(wide * wide, axis=-1, keepdims=True) + epsilon)


def weights_of(q, k, causal):
    length = k.shape[0]
    powers = jnp.exp(dot(stacked(q), k, NT) * (1.0 / math.sqrt(SIZE)))
    if causal:
        query = lax.broadcasted_iota(jnp.int32, powers.shape, 0) % length
        key = lax.broadcasted_iota(jnp.int32, powers.shape, 1)
        powers = jnp.where(query >= key, powers, 0.0)
    return powers / jnp.sum(powers, axis=-1, keepdims=True)


def attend_forward(packed, mixed, weights, begin, end, causal):
    length = weights.shape[3]
    width = mixed.shape[1]

    def one(n, carry):
        rows = pl.ds(pl.multiple_of(n * length, 16), length)
        for p in range(width // PAIR):
            lanes = p * PAIR
            q = packed[rows, lanes : lanes + PAIR]
            k = packed[rows, width + lanes : width + lanes + PAIR]
            v = packed[rows, 2 * width + lanes : 2 * width + lanes + PAIR]
            w = weights_of(q, k, causal).astype(jnp.bfloat16)
            weights[n, p] = w
            mixed[rows, lanes : lanes + PAIR] = unstacked(dot(w, v)).astype(jnp.bfloat16)
        return carry

    lax.fori_loop(begin, end, one, 0)


def attend_backward(packed, weights, d_mixed, d_packed, begin, end):
    length = weights.shape[3]
    width = d_mixed.shape[1]

    def one(n, carry):
        rows = pl.ds(pl.multiple_of(n * length, 16), length)
        for p in range(width // PAIR):
            lanes = p * PAIR
            q = packed[rows, lanes : lanes + PAIR]
            k = packed[rows, width + lanes : width + lanes + PAIR]
            v = packed[rows, 2 * width + lanes : 2 * width + lanes + PAIR]
            up = stacked(d_mixed[rows, lanes : lanes + PAIR])
            w = weights[n, p]
            wide = w.astype(jnp.float32)
            d_w = dot(up, v, NT).astype(jnp.bfloat16).astype(jnp.float32)
            d_scores = wide * (d_w - jnp.sum(d_w * wide, axis=-1, keepdims=True))
            d_scores = (d_scores * (1.0 / math.sqrt(SIZE))).astype(jnp.bfloat16)
            d_q = unstacked(dot(d_scores, k))
            d_k = dot(d_scores, stacked(q), TN)
            d_v = dot(w, up, TN)
            d_packed[rows, lanes : lanes + PAIR] = d_q.astype(jnp.bfloat16)
            d_packed[rows, width + lanes : width + lanes + PAIR] = d_k.astype(jnp.bfloat16)
            d_packed[rows, 2 * width + lanes : 2 * width + lanes + PAIR] = d_v.astype(jnp.bfloat16)
        return carry

    lax.fori_loop(begin, end, one, 0)


def selected(targets, rows, values):
    onehot = jnp.where(targets == lax.broadcasted_iota(jnp.int32, (rows, values.shape[0]), 0), 1.0, 0.0)
    return dot(onehot.astype(jnp.bfloat16), values)


def packed_rows(wire, at, values, block):
    rows, width = wire.shape[0], values.shape[1]
    tokens = values.shape[0]
    half = width // 2
    wire[:, :width] = selected(at[0:1, :tokens], rows, values).astype(jnp.bfloat16)
    low = selected(at[1:2, :tokens], rows, values[:, :half])
    high = selected(at[2:3, :tokens], rows, values[:, half:])
    wire[:, width:] = (low + high).astype(jnp.bfloat16)


def unpacked_rows(wire, at, tokens, width):
    rows = wire.shape[0]
    main = selected(at[0:1, :rows], tokens, wire[:, :width])
    low = selected(at[1:2, :rows], tokens, wire[:, width:])
    high = selected(at[2:3, :rows], tokens, wire[:, width:])
    return (main + jnp.concatenate([low, high], axis=1)).astype(jnp.bfloat16)


def routes(slots, count, feeders):
    device, slot, feeder = np.meshgrid(np.arange(count), np.arange(slots), np.arange(feeders), indexing="ij")
    place = slot * feeders + feeder
    tokens, rows = slots * count * feeders, count * 8
    found = []
    for order in (feeder * count * slots + device * slots + slot, slot * count * feeders + device * feeders + feeder):
        to, back = np.full((3, tokens), -1), np.full((3, tokens), -1)
        for kind, mine, row in (
            (0, place < 8, device * 8 + place),
            (1, place >= 8, device * 8 + place - 8),
            (2, place >= 8, device * 8 + place - 8 + (slots * feeders - 8)),
        ):
            to[kind, order[mine]] = row[mine]
            back[kind, row[mine]] = order[mine]
        found.append((to, back))
    assert 8 + 2 * (slots * feeders - 8) == 16
    (time_to, time_back), (feed_to, feed_back) = found
    table = np.full((32, tokens), -1)
    for n, rows in enumerate((time_to, feed_back, feed_to, time_back)):
        table[8 * n : 8 * n + 3] = rows
    return table.astype(np.int32)


def gradient_part(g, to, total):
    width = total.shape[0]
    slabs = width // LANES
    for slab in range(slabs):
        first = (to * slabs + slab) * width
        g[first : first + width, :] = total[:, slab * LANES : (slab + 1) * LANES].astype(jnp.bfloat16)


def step_kernel(
    batch, count,
    x_ref, row_ref, table_ref, time_qkv, time_out, feed_qkv_ref, feed_out_ref, route_ref, up_ref, partner_ref,
    load_ref, time_mean_ref, feed_mean_ref,
    feed_qkv, feed_out, adjoint,
    first, t_normed, t_packed, t_weights, t_mixed, f_normed, f_packed, f_weights, f_mixed,
    hidden, d_mixed, d_packed, sent, got, back, returned,
    t_g, t_inbox, t_pair, t_full, f_g, f_inbox, f_pair, f_full,
    wire_send, wire_recv, own_sem, fetch_sem, *sems,
):
    sequences, length, width = x_ref.shape
    feeders = sequences // batch
    groups = f_weights.shape[0] // batch
    tokens = feeders * length
    place = Place()
    greet(place, count)
    fetches = [
        pltpu.make_async_copy(source, target, fetch_sem.at[n])
        for n, (source, target) in enumerate(((feed_qkv_ref, feed_qkv), (feed_out_ref, feed_out), (up_ref, adjoint)))
    ]
    for fetch in fetches:
        fetch.start()
    t_sum = Reduction(place, partner_ref, t_g, t_inbox, t_pair, t_full, time_mean_ref, sems[:7])
    f_sum = Reduction(place, partner_ref, f_g, f_inbox, f_pair, f_full, feed_mean_ref, sems[7:])
    there, home = [], []
    for b in range(batch):
        pairs = ((there, sent, got, b), (home, back, returned, batch + b))
        for exchanges, source, target, n in pairs:
            exchanges.append(
                Exchange(count, source.at[b], target.at[b], wire_send.at[n], wire_recv.at[n], own_sem.at[n])
            )
    part_rows = 4 * width
    table_rows = table_ref.shape[0]
    onehot = (row_ref[...] == lax.broadcasted_iota(jnp.int32, (row_ref.shape[0], table_rows), 1)).astype(jnp.bfloat16)
    added = dot(onehot, table_ref[...])

    def time_forward(b):
        here = slice(b * tokens, (b + 1) * tokens)
        for n in range(feeders):
            rows = slice(b * tokens + n * length, b * tokens + (n + 1) * length)
            start = x_ref[b * feeders + n].astype(jnp.float32) + added[n : n + 1]
            first[rows, :] = start
            t_normed[rows, :] = (start * norm_factor(start)).astype(jnp.bfloat16)
        t_packed[here, :] = dot(t_normed[here, :], time_qkv[...]).astype(jnp.bfloat16)
        attend_forward(t_packed, t_mixed, t_weights, b * feeders, (b + 1) * feeders, True)
        result = (first[here, :] + dot(t_mixed[here, :], time_out[...])).astype(jnp.bfloat16)
        packed_rows(sent.at[b], route_ref[0:8, :], result, count)

    def feed_layer(b):
        here = slice(b * tokens, (b + 1) * tokens)
        hidden[here, :] = unpacked_rows(got[b], route_ref[8:16, :], tokens, width)
        wide = hidden[here, :].astype(jnp.float32)
        f_normed[here, :] = (wide * norm_factor(wide)).astype(jnp.bfloat16)
        f_packed[here, :] = dot(f_normed[here, :], feed_qkv[...]).astype(jnp.bfloat16)
        attend_forward(f_packed, f_mixed, f_weights, b * groups, (b + 1) * groups, False)
        result = hidden[here, :].astype(jnp.float32) + dot(f_mixed[here, :], feed_out[...])
        load_ref[b * groups : (b + 1) * groups] = result.astype(jnp.bfloat16).reshape(groups, -1, width)
        d_mixed[here, :] = dot(adjoint[here, :], feed_out[...], NT).astype(jnp.bfloat16)
        attend_backward(f_packed, f_weights, d_mixed, d_packed, b * groups, (b + 1) * groups)
        g = dot(d_packed[here, :], feed_qkv[...], NT).astype(jnp.bfloat16).astype(jnp.float32)
        wide = hidden[here, :].astype(jnp.float32)
        factor = norm_factor(wide)
        along = jnp.sum(g * wide, axis=-1, keepdims=True) * (factor * factor * factor) * (1.0 / width)
        d_hidden = (g * factor - wide * along).astype(jnp.bfloat16)
        total = (d_hidden.astype(jnp.float32) + adjoint[here, :].astype(jnp.float32)).astype(jnp.bfloat16)
        packed_rows(back.at[b], route_ref[16:24, :], total, count)

    def time_upstream(b):
        here = slice(b * tokens, (b + 1) * tokens)
        hidden[here, :] = unpacked_rows(returned[b], route_ref[24:32, :], tokens, width)

    def time_backward(b):
        here = slice(b * tokens, (b + 1) * tokens)
        d_mixed[here, :] = dot(hidden[here, :], time_out[...], NT).astype(jnp.bfloat16)
        attend_backward(t_packed, t_weights, d_mixed, d_packed, b * feeders, (b + 1) * feeders)

    for b in range(batch):
        time_forward(b)
        if b == 0:
            all_greeted(count)
        there[b].start()
    for fetch in fetches:
        fetch.wait()
    for b in range(batch):
        there[b].wait()
        feed_layer(b)
        home[b].start()

    early = range(4)
    for part in early:
        if part < 3:
            f_total = dot(f_normed[...], d_packed[:, part * width : (part + 1) * width], TN)
        else:
            f_total = dot(f_mixed[...], adjoint[...], TN)
        gradient_part(f_g, part, f_total)
        f_sum.start(part * part_rows, (part + 1) * part_rows)
    for b in range(batch):
        home[b].wait()
        time_upstream(b)
        if b == batch - 1:
            gradient_part(f_g, 4, dot(t_mixed[...], hidden[...], TN))
            f_sum.start(4 * part_rows, 5 * part_rows)
        time_backward(b)
        f_sum.turn(b, early)
    for part in range(3):
        gradient_part(t_g, part, dot(t_normed[...], d_packed[:, part * width : (part + 1) * width], TN))
        t_sum.start(part * part_rows, (part + 1) * part_rows)
        if part == 0:
            f_sum.turn(0, (4,))
    f_sum.turn(batch, early)
    f_sum.turn(1, (4,))
    for turn in range(TURNS):
        t_sum.turn(turn)
        f_sum.turn(turn + batch + 1, early)
        f_sum.turn(turn + 2, (4,))
    f_sum.finish()
    t_sum.finish()


def finish_kernel(time_ref, feed_ref, out_ref, held, wide, in_sem, out_sem):
    slabs, depth, lanes = time_ref.shape[1:]
    rows = 4 * depth

    def get(n):
        layer, slab = n // slabs, n % slabs
        if layer:
            pieces = ((feed_ref.at[pl.ds(0, 4), slab], held.at[n]),)
        else:
            pieces = (
                (time_ref.at[:, slab], held.at[n, pl.ds(0, 3)]),
                (feed_ref.at[4, slab], held.at[n, 3]),
            )
        return [pltpu.make_async_copy(*piece, in_sem.at[n, i]) for i, piece in enumerate(pieces)]

    def put(n):
        target = out_ref.at[pl.ds(n // slabs * rows, rows), pl.ds(n % slabs * lanes, lanes)]
        return pltpu.make_async_copy(wide.at[n], target, out_sem.at[n])

    for n in range(2 * slabs):
        for copy in get(n):
            copy.start()
    for n in range(2 * slabs):
        for copy in get(n):
            copy.wait()
        for part in range(3):
            wide[n, pl.ds(part, depth, stride=3), :] = held[n, part].astype(jnp.float32)
        wide[n, 3 * depth :, :] = held[n, 3].astype(jnp.float32)
        put(n).start()
    for n in range(2 * slabs):
        put(n).wait()


def finished(time_mean, feed_mean):
    slabs, depth, lanes = time_mean.shape[1:]
    rows = 4 * depth
    return pl.pallas_call(
        finish_kernel,
        out_shape=jax.ShapeDtypeStruct((2 * rows, slabs * lanes), jnp.float32),
        in_specs=[ANY, ANY],
        out_specs=ANY,
        scratch_shapes=[
            pltpu.VMEM((2 * slabs, 4, depth, lanes), jnp.bfloat16),
            pltpu.VMEM((2 * slabs, rows, lanes), jnp.float32),
            pltpu.SemaphoreType.DMA((2 * slabs, 2)),
            pltpu.SemaphoreType.DMA((2 * slabs,)),
        ],
        compiler_params=pltpu.CompilerParams(vmem_limit_bytes=60 * 1024 * 1024),
    )(time_mean, feed_mean)


VMEM = pl.BlockSpec(memory_space=pltpu.VMEM)
ANY = pl.BlockSpec(memory_space=pl.ANY)


def on_device(
    measured_features,
    feeder_of_row,
    feeder_table,
    time_qkv,
    time_out,
    feed_qkv,
    feed_out,
    adjoint_of_prediction,
    round_index,
):
    batch, feed_local, slot_count, width = measured_features.shape
    feeder_count = adjoint_of_prediction.shape[1]
    slot_local = adjoint_of_prediction.shape[2]
    count = feeder_count // feed_local
    rows = batch * feed_local * slot_count
    pairs = width // PAIR
    bf16 = jnp.bfloat16
    sequences, groups = batch * feed_local, batch * slot_local

    route = jnp.asarray(routes(slot_local, count, feed_local))
    row_column = jnp.pad(feeder_of_row, (0, 8 - feed_local)).reshape(8, 1)
    partner = jnp.broadcast_to(round_index.astype(jnp.float32), (8, LANES))
    upstream = jnp.transpose(adjoint_of_prediction, (0, 2, 1, 3)).reshape(rows, width)
    part_rows = width * width // LANES
    time_rows, feed_rows = 3 * part_rows, 5 * part_rows
    chains = len(LINKS)

    def held(*shape):
        return pltpu.VMEM(shape, bf16)

    def reduction(n):
        return [held(n, LANES), held(n, LANES), held(len(PAIRS), n >> len(LINKS), LANES), held(n, LANES)]

    def semaphores():
        steps = [COPIES, COPIES, len(PAIRS), len(PAIRS), COPIES, COPIES]
        return [pltpu.SemaphoreType.DMA((chains, s)) for s in steps] + [pltpu.SemaphoreType.DMA((chains,))]

    wire = held(batch, count * 8, width + width // 2)
    load, time_mean, feed_mean = pl.pallas_call(
        partial(step_kernel, batch, count),
        out_shape=(
            jax.ShapeDtypeStruct((groups, feeder_count, width), bf16),
            jax.ShapeDtypeStruct((time_rows, LANES), bf16),
            jax.ShapeDtypeStruct((feed_rows, LANES), bf16),
        ),
        in_specs=[VMEM, VMEM, VMEM, VMEM, VMEM, ANY, ANY, VMEM, ANY, VMEM],
        out_specs=(VMEM, ANY, ANY),
        scratch_shapes=[
            held(width, 3 * width),
            held(width, width),
            held(rows, width),
            pltpu.VMEM((rows, width), jnp.float32),
            held(rows, width),
            held(rows, 3 * width),
            held(sequences, pairs, 2 * slot_count, slot_count),
            held(rows, width),
            held(rows, width),
            held(rows, 3 * width),
            held(groups, pairs, 2 * feeder_count, feeder_count),
            held(rows, width),
            held(rows, width),
            held(rows, width),
            held(rows, 3 * width),
            wire,
            wire,
            wire,
            wire,
        ]
        + reduction(time_rows)
        + reduction(feed_rows)
        + [pltpu.SemaphoreType.DMA((2 * batch, count))] * 2
        + [pltpu.SemaphoreType.DMA((2 * batch,)), pltpu.SemaphoreType.DMA((3,))]
        + semaphores()
        + semaphores(),
        compiler_params=pltpu.CompilerParams(collective_id=1, has_side_effects=True, vmem_limit_bytes=60 * 1024 * 1024),
    )(
        measured_features.reshape(sequences, slot_count, width),
        row_column,
        feeder_table,
        time_qkv,
        time_out,
        feed_qkv,
        feed_out,
        route,
        upstream,
        partner,
    )
    predicted_load = jnp.transpose(load.reshape(batch, slot_local, feeder_count, width), (0, 2, 1, 3))
    slabs = (width // LANES, width, LANES)
    gradients = finished(time_mean.reshape(3, *slabs), feed_mean.reshape(5, *slabs))
    return (predicted_load, gradients[None])


def solution(mesh):
    placed = (
        P("gossip", "field", None, None),
        P("field"),
        P(),
        P(),
        P(),
        P(),
        P(),
        P("gossip", None, "field", None),
        P(),
    )
    return jax.shard_map(
        on_device,
        mesh=mesh,
        in_specs=placed,
        out_specs=(P("gossip", None, "field", None), P("gossip", None, None)),
        check_vma=False,
    )
```

profile of v0, /device:TPU:0, one launch (start us, length us, event | category | flops | bytes accessed | tf_op | source)
XLA Modules:
  0.0 128.4 jit_solution(15899551796054377116)
XLA Ops:
  1.3 0.7 pad_bitcast_fusion
  1.9 0.7 copy.12.row_ref
  2.6 0.6 broadcast_in_dim.8.partner_ref
  3.2 119.6 %shard_map.113 = (bf16[6,128,512]{2,1,0:T(8,128)(2,1)}, bf16[6144,128]{1,0:T(8,128)(2,1)}, bf16[10240,128]{1,0:T(8,128)(2,1)}) custom-call(bf16[8,96,512]{2,1,0:T(8,128)(2,1)} %bitcast.17, s32[8,1]{1,0:T(8,128)} %copy.12.row_ref, bf16[128,512]{1,0:T(8,128)(2,1)} %table_ref.1, bf16[512,1536]{1,0:T(8,128)(2,1)} %time_qkv.1, bf16[512,512]{1,0:T(8,128)(2,1)} %time_out.1, ...), custom_call_target="tpu_custom_call" | custom-call | tf_op jit(solution)/shard_map/pallas_call | solution.py:635
  122.8 0.0 copy-start
  122.8 4.7 %shard_map.114 = f32[4096,512]{1,0:T(8,128)} custom-call(bf16[3,4,512,128]{3,2,1,0:T(8,128)(2,1)} %bitcast.15, bf16[5,4,512,128]{3,2,1,0:T(8,128)(2,1)} %bitcast.14), custom_call_target="tpu_custom_call" | custom-call | tf_op jit(solution)/shard_map/pallas_call | solution.py:577
  127.5 0.0 copy-done
  127.5 0.9 copy.15
Async XLA Ops:
  122.8 4.7 %copy-start = (bf16[6,128,512]{2,1,0:T(8,128)(2,1)S(1)}, bf16[6,128,512]{2,1,0:T(8,128)(2,1)}, u32[]{:S(2)}) copy-start(bf16[6,128,512]{2,1,0:T(8,128)(2,1)} %get-tuple-element.5) | copy-start | bytes 2359300
where the time goes:
time: 129 us; the launch traced here: 128 us
  Pallas kernels  124 us (96%)
  local copies, waits for them, and re-layouts  2.81 us (2%)
  between operations  1.31 us (1%)
    pallas_call x1, Pallas kernels, on_device(): pl.pallas_call(partial(step_kernel, batch, count), out_shape=(jax.ShapeDt...  120 us
    pallas_call x1, Pallas kernels, finished(): pl.pallas_call(finish_kernel, out_shape=jax.ShapeDtypeStruct((2 * rows, s...  4.67 us

commit v1 on v0

--- a/solution.py
+++ b/solution.py
@@ -16,10 +16,19 @@
 LANES = 128
 LINKS = ("ya", "za", "xa", "yb", "zb")
 PAIRS = ("core", "xb")
-GROUPS = (1, 2, 2)
+GROUPS = (1, 1, 1, 2)
 STEPS = len(GROUPS)
 TURNS = 2 * STEPS + 1
 COPIES = sum(2**size - 1 for size in GROUPS)
+
+ORDER = (
+    100, 110, 120, 130, 140, 20, 0, 10, 121, 131, 111, 141, 101, 30, 40, 21,
+    122, 132, 1, 11, 112, 142, 102, 31, 41, 22, 123, 12, 133, 2, 113, 32,
+    42, 143, 103, 124, 23, 134, 13, 114, 3, 144, 33, 43, 104, 24, 14, 125,
+    4, 135, 34, 115, 44, 145, 25, 105, 15, 126, 136, 35, 5, 26, 116, 146,
+    45, 16, 106, 36, 6, 137, 127, 46, 27, 147, 117, 37, 107, 17, 47, 7,
+    138, 128, 148, 118, 38, 108, 28, 48, 18, 8,
+)
 
 
 class Place:
@@ -507,8 +516,7 @@
         feed_layer(b)
         home[b].start()
 
-    early = range(4)
-    for part in early:
+    for part in range(4):
         if part < 3:
             f_total = dot(f_normed[...], d_packed[:, part * width : (part + 1) * width], TN)
         else:
@@ -522,18 +530,12 @@
             gradient_part(f_g, 4, dot(t_mixed[...], hidden[...], TN))
             f_sum.start(4 * part_rows, 5 * part_rows)
         time_backward(b)
-        f_sum.turn(b, early)
+    f_sum.turn(0, ())
     for part in range(3):
         gradient_part(t_g, part, dot(t_normed[...], d_packed[:, part * width : (part + 1) * width], TN))
         t_sum.start(part * part_rows, (part + 1) * part_rows)
-        if part == 0:
-            f_sum.turn(0, (4,))
-    f_sum.turn(batch, early)
-    f_sum.turn(1, (4,))
-    for turn in range(TURNS):
-        t_sum.turn(turn)
-        f_sum.turn(turn + batch + 1, early)
-        f_sum.turn(turn + 2, (4,))
+    for code in ORDER:
+        (f_sum if code >= 100 else t_sum).advance(code // 10 % 10, code % 10)
     f_sum.finish()
     t_sum.finish()
 

time: 129 us -> 118 us (0.915)
  Pallas kernels: 124 us -> 113 us
    pallas_call x1, Pallas kernels: 120 us -> 108 us  [on_device(): pl.pallas_call(partial(step_kernel, batch, count), out_shape=(jax.ShapeDt...]
where the time goes in v1:
time: 118 us; the launch traced here: 117 us
  Pallas kernels  113 us (96%)
  local copies, waits for them, and re-layouts  2.81 us (2%)
  between operations  1.31 us (1%)
    pallas_call x1, Pallas kernels, on_device(): pl.pallas_call(partial(step_kernel, batch, count), out_shape=(jax.ShapeDt...  108 us
    pallas_call x1, Pallas kernels, finished(): pl.pallas_call(finish_kernel, out_shape=jax.ShapeDtypeStruct((2 * rows, s...  4.67 us

profile of v1, /device:TPU:0, one launch (start us, length us, event | category | flops | bytes accessed | tf_op | source)
XLA Modules:
  0.0 117.1 jit_solution(1864885893297010517)
XLA Ops:
  1.3 0.7 pad_bitcast_fusion
  1.9 0.7 copy.12.row_ref
  2.6 0.6 broadcast_in_dim.8.partner_ref
  3.2 108.3 %shard_map.113 = (bf16[6,128,512]{2,1,0:T(8,128)(2,1)}, bf16[6144,128]{1,0:T(8,128)(2,1)}, bf16[10240,128]{1,0:T(8,128)(2,1)}) custom-call(bf16[8,96,512]{2,1,0:T(8,128)(2,1)} %bitcast.17, s32[8,1]{1,0:T(8,128)} %copy.12.row_ref, bf16[128,512]{1,0:T(8,128)(2,1)} %table_ref.1, bf16[512,1536]{1,0:T(8,128)(2,1)} %time_qkv.1, bf16[512,512]{1,0:T(8,128)(2,1)} %time_out.1, ...), custom_call_target="tpu_custom_call" | custom-call | tf_op jit(solution)/shard_map/pallas_call | solution.py:637
  111.5 0.0 copy-start
  111.5 4.7 %shard_map.114 = f32[4096,512]{1,0:T(8,128)} custom-call(bf16[3,4,512,128]{3,2,1,0:T(8,128)(2,1)} %bitcast.15, bf16[5,4,512,128]{3,2,1,0:T(8,128)(2,1)} %bitcast.14), custom_call_target="tpu_custom_call" | custom-call | tf_op jit(solution)/shard_map/pallas_call | solution.py:579
  116.2 0.0 copy-done
  116.2 0.9 copy.15
Async XLA Ops:
  111.5 4.7 %copy-start = (bf16[6,128,512]{2,1,0:T(8,128)(2,1)S(1)}, bf16[6,128,512]{2,1,0:T(8,128)(2,1)}, u32[]{:S(2)}) copy-start(bf16[6,128,512]{2,1,0:T(8,128)(2,1)} %get-tuple-element.5) | copy-start | bytes 2359300

commit v2 on v1

--- a/solution.py
+++ b/solution.py
@@ -20,14 +20,46 @@
 STEPS = len(GROUPS)
 TURNS = 2 * STEPS + 1
 COPIES = sum(2**size - 1 for size in GROUPS)
+TIME_PLAN = (
+    (1, (3, 2, 4, 1, 0)),
+    (2, (1, 4, 0, 3, 2)),
+    (1, (4, 0, 2, 3, 1)),
+    (2, (4, 0, 2, 3, 1)),
+    (2, (3, 1, 0, 4, 2)),
+    (2, (0, 3, 4, 2, 1)),
+    (1, (3, 1, 4, 0, 2)),
+    (1, (0, 2, 4, 3, 1)),
+)
+FEED_PLAN = (
+    (3, (2, 1, 3, 4, 0)),
+    (2, (2, 3, 1, 0, 4)),
+    (1, (0, 4, 1, 3, 2)),
+    (2, (4, 0, 3, 2, 1)),
+    (1, (1, 0, 3, 2, 4)),
+    (1, (3, 2, 4, 0, 1)),
+    (3, (0, 2, 4, 1, 3)),
+    (3, (1, 2, 3, 0, 4)),
+    (2, (3, 2, 1, 0, 4)),
+    (2, (4, 1, 0, 3, 2)),
+)
 
 ORDER = (
-    100, 110, 120, 130, 140, 20, 0, 10, 121, 131, 111, 141, 101, 30, 40, 21,
-    122, 132, 1, 11, 112, 142, 102, 31, 41, 22, 123, 12, 133, 2, 113, 32,
-    42, 143, 103, 124, 23, 134, 13, 114, 3, 144, 33, 43, 104, 24, 14, 125,
-    4, 135, 34, 115, 44, 145, 25, 105, 15, 126, 136, 35, 5, 26, 116, 146,
-    45, 16, 106, 36, 6, 137, 127, 46, 27, 147, 117, 37, 107, 17, 47, 7,
-    138, 128, 148, 118, 38, 108, 28, 48, 18, 8,
+    (),
+    (120, 140, 150),
+    (130,),
+    (100, 180),
+    (
+        160, 170, 190, 121, 141, 110, 151, 0, 20, 131, 10, 181, 30, 40, 152, 101,
+        161, 50, 60, 142, 191, 70, 122, 11, 171, 21, 111, 182, 1, 132, 31, 41,
+        162, 102, 61, 153, 192, 143, 71, 51, 12, 22, 112, 2, 123, 172, 183, 32,
+        133, 42, 154, 144, 163, 62, 72, 103, 193, 52, 124, 13, 23, 184, 134, 113,
+        3, 173, 33, 164, 43, 155, 104, 145, 194, 63, 73, 14, 24, 53, 125, 114,
+        4, 185, 174, 135, 34, 44, 156, 146, 64, 74, 165, 54, 105, 195, 126, 15,
+        25, 115, 186, 5, 136, 175, 157, 45, 147, 35, 75, 166, 65, 196, 55, 106,
+        26, 127, 16, 116, 6, 187, 176, 137, 76, 36, 46, 66, 148, 158, 56, 27,
+        197, 167, 17, 117, 7, 128, 107, 37, 177, 138, 47, 188, 77, 67, 28, 57,
+        8, 118, 18, 168, 198, 78, 48, 38, 68, 108, 178, 58,
+    ),
 )
 
 
@@ -61,17 +93,13 @@
         return (at["x_hi"] * 2 + at["core"], (at["x_lo"] * 4 + at["z"]) * 4 + at["y"])
 
 
-def chains_of(rows):
-    unit = 512
-    count, more = divmod(rows // unit, len(LINKS))
+def chains_of(plan):
     chains, first = [], 0
-    for turn in range(len(LINKS)):
-        names = [LINKS[(turn + s) % len(LINKS)] for s in range(len(LINKS))]
+    for units, turns in plan:
+        names = [LINKS[turn] for turn in turns]
         groups = tuple(tuple(names[sum(GROUPS[:s]) : sum(GROUPS[: s + 1])]) for s in range(STEPS))
-        size = (count + (turn < more)) * unit
-        chains.append((first, size, groups))
-        first += size
-    assert first == rows
+        chains.append((first, units * 512, groups))
+        first += units * 512
     return chains
 
 
@@ -83,11 +111,12 @@
 
 
 class Reduction:
-    def __init__(self, place, partner, g, inbox, pairbox, full, out, sems):
+    def __init__(self, plan, place, partner, g, inbox, pairbox, full, out, sems):
         self.place, self.partner = place, partner
         self.g, self.inbox, self.pairbox, self.full, self.out = g, inbox, pairbox, full, out
         self.rs_send, self.rs_recv, self.pair_send, self.pair_recv, self.ag_send, self.ag_recv, self.out_sem = sems
-        self.chains = chains_of(g.shape[0])
+        self.chains = chains_of(plan)
+        assert sum(rows for first, rows, groups in self.chains) == g.shape[0]
         self.at = []
         self.steps = []
         for first, rows, groups in self.chains:
@@ -193,11 +222,6 @@
                 for copy in self.rs_copies(j, 0):
                     copy.start()
 
-    def turn(self, t, chains=None):
-        if 0 <= t < TURNS:
-            for j in range(len(self.chains)) if chains is None else chains:
-                self.advance(j, t)
-
     def advance(self, j, stage):
         following = []
         if stage < STEPS:
@@ -450,8 +474,8 @@
     ]
     for fetch in fetches:
         fetch.start()
-    t_sum = Reduction(place, partner_ref, t_g, t_inbox, t_pair, t_full, time_mean_ref, sems[:7])
-    f_sum = Reduction(place, partner_ref, f_g, f_inbox, f_pair, f_full, feed_mean_ref, sems[7:])
+    t_sum = Reduction(TIME_PLAN, place, partner_ref, t_g, t_inbox, t_pair, t_full, time_mean_ref, sems[:7])
+    f_sum = Reduction(FEED_PLAN, place, partner_ref, f_g, f_inbox, f_pair, f_full, feed_mean_ref, sems[7:])
     there, home = [], []
     for b in range(batch):
         pairs = ((there, sent, got, b), (home, back, returned, batch + b))
@@ -504,6 +528,10 @@
         d_mixed[here, :] = dot(hidden[here, :], time_out[...], NT).astype(jnp.bfloat16)
         attend_backward(t_packed, t_weights, d_mixed, d_packed, b * feeders, (b + 1) * feeders)
 
+    def advance(codes):
+        for code in codes:
+            (f_sum if code >= 100 else t_sum).advance(code // 10 % 10, code % 10)
+
     for b in range(batch):
         time_forward(b)
         if b == 0:
@@ -530,12 +558,13 @@
             gradient_part(f_g, 4, dot(t_mixed[...], hidden[...], TN))
             f_sum.start(4 * part_rows, 5 * part_rows)
         time_backward(b)
-    f_sum.turn(0, ())
+        advance(ORDER[b])
     for part in range(3):
         gradient_part(t_g, part, dot(t_normed[...], d_packed[:, part * width : (part + 1) * width], TN))
         t_sum.start(part * part_rows, (part + 1) * part_rows)
-    for code in ORDER:
-        (f_sum if code >= 100 else t_sum).advance(code // 10 % 10, code % 10)
+        if part < 2:
+            advance(ORDER[batch + part])
+    advance(ORDER[4])
     f_sum.finish()
     t_sum.finish()
 
@@ -621,7 +650,6 @@
     upstream = jnp.transpose(adjoint_of_prediction, (0, 2, 1, 3)).reshape(rows, width)
     part_rows = width * width // LANES
     time_rows, feed_rows = 3 * part_rows, 5 * part_rows
-    chains = len(LINKS)
 
     def held(*shape):
         return pltpu.VMEM(shape, bf16)
@@ -629,7 +657,7 @@
     def reduction(n):
         return [held(n, LANES), held(n, LANES), held(len(PAIRS), n >> len(LINKS), LANES), held(n, LANES)]
 
-    def semaphores():
+    def semaphores(chains):
         steps = [COPIES, COPIES, len(PAIRS), len(PAIRS), COPIES, COPIES]
         return [pltpu.SemaphoreType.DMA((chains, s)) for s in steps] + [pltpu.SemaphoreType.DMA((chains,))]
 
@@ -668,8 +696,8 @@
         + reduction(feed_rows)
         + [pltpu.SemaphoreType.DMA((2 * batch, count))] * 2
         + [pltpu.SemaphoreType.DMA((2 * batch,)), pltpu.SemaphoreType.DMA((3,))]
-        + semaphores()
-        + semaphores(),
+        + semaphores(len(TIME_PLAN))
+        + semaphores(len(FEED_PLAN)),
         compiler_params=pltpu.CompilerParams(collective_id=1, has_side_effects=True, vmem_limit_bytes=60 * 1024 * 1024),
     )(
         measured_features.reshape(sequences, slot_count, width),

time: 118 us -> 115 us (0.975)
  Pallas kernels: 113 us -> 111 us
    pallas_call x1, Pallas kernels: 108 us -> 106 us  [on_device(): pl.pallas_call(partial(step_kernel, batch, count), out_shape=(jax.ShapeDt...]
where the time goes in v2:
time: 115 us
  Pallas kernels  111 us (97%)
  local copies, waits for them, and re-layouts  2.81 us (2%)
  between operations  1.31 us (1%)
    pallas_call x1, Pallas kernels, on_device(): pl.pallas_call(partial(step_kernel, batch, count), out_shape=(jax.ShapeDt...  106 us
    pallas_call x1, Pallas kernels, finished(): pl.pallas_call(finish_kernel, out_shape=jax.ShapeDtypeStruct((2 * rows, s...  4.67 us

profile of v2, /device:TPU:0, one launch (start us, length us, event | category | flops | bytes accessed | tf_op | source)
XLA Modules:
  0.0 115.1 jit_solution(16248247062367155704)
XLA Ops:
  1.3 0.7 pad_bitcast_fusion
  1.9 0.7 copy.12.row_ref
  2.6 0.6 broadcast_in_dim.8.partner_ref
  3.2 106.3 %shard_map.113 = (bf16[6,128,512]{2,1,0:T(8,128)(2,1)}, bf16[6144,128]{1,0:T(8,128)(2,1)}, bf16[10240,128]{1,0:T(8,128)(2,1)}) custom-call(bf16[8,96,512]{2,1,0:T(8,128)(2,1)} %bitcast.17, s32[8,1]{1,0:T(8,128)} %copy.12.row_ref, bf16[128,512]{1,0:T(8,128)(2,1)} %table_ref.1, bf16[512,1536]{1,0:T(8,128)(2,1)} %time_qkv.1, bf16[512,512]{1,0:T(8,128)(2,1)} %time_out.1, ...), custom_call_target="tpu_custom_call" | custom-call | tf_op jit(solution)/shard_map/pallas_call | solution.py:665
  109.6 0.0 copy-start
  109.6 4.7 %shard_map.114 = f32[4096,512]{1,0:T(8,128)} custom-call(bf16[3,4,512,128]{3,2,1,0:T(8,128)(2,1)} %bitcast.15, bf16[5,4,512,128]{3,2,1,0:T(8,128)(2,1)} %bitcast.14), custom_call_target="tpu_custom_call" | custom-call | tf_op jit(solution)/shard_map/pallas_call | solution.py:608
  114.2 0.0 copy-done
  114.3 0.9 copy.15
Async XLA Ops:
  109.6 4.7 %copy-start = (bf16[6,128,512]{2,1,0:T(8,128)(2,1)S(1)}, bf16[6,128,512]{2,1,0:T(8,128)(2,1)}, u32[]{:S(2)}) copy-start(bf16[6,128,512]{2,1,0:T(8,128)(2,1)} %get-tuple-element.5) | copy-start | bytes 2359300

commit v3 on v2

--- a/solution.py
+++ b/solution.py
@@ -20,45 +20,46 @@
 STEPS = len(GROUPS)
 TURNS = 2 * STEPS + 1
 COPIES = sum(2**size - 1 for size in GROUPS)
+
 TIME_PLAN = (
-    (1, (3, 2, 4, 1, 0)),
-    (2, (1, 4, 0, 3, 2)),
-    (1, (4, 0, 2, 3, 1)),
-    (2, (4, 0, 2, 3, 1)),
     (2, (3, 1, 0, 4, 2)),
-    (2, (0, 3, 4, 2, 1)),
-    (1, (3, 1, 4, 0, 2)),
-    (1, (0, 2, 4, 3, 1)),
+    (2, (2, 0, 1, 3, 4)),
+    (1, (1, 2, 3, 4, 0)),
+    (2, (1, 0, 3, 2, 4)),
+    (1, (3, 4, 1, 0, 2)),
+    (1, (4, 3, 1, 2, 0)),
+    (2, (2, 4, 3, 0, 1)),
+    (1, (0, 3, 1, 4, 2)),
 )
 FEED_PLAN = (
-    (3, (2, 1, 3, 4, 0)),
-    (2, (2, 3, 1, 0, 4)),
-    (1, (0, 4, 1, 3, 2)),
-    (2, (4, 0, 3, 2, 1)),
-    (1, (1, 0, 3, 2, 4)),
-    (1, (3, 2, 4, 0, 1)),
-    (3, (0, 2, 4, 1, 3)),
-    (3, (1, 2, 3, 0, 4)),
-    (2, (3, 2, 1, 0, 4)),
-    (2, (4, 1, 0, 3, 2)),
+    (1, (0, 1, 3, 2, 4)),
+    (2, (2, 4, 3, 0, 1)),
+    (1, (3, 1, 2, 0, 4)),
+    (3, (1, 4, 0, 3, 2)),
+    (3, (0, 3, 1, 4, 2)),
+    (3, (4, 0, 3, 2, 1)),
+    (2, (4, 2, 3, 0, 1)),
+    (1, (0, 3, 4, 2, 1)),
+    (2, (3, 4, 2, 1, 0)),
+    (2, (2, 1, 0, 3, 4)),
 )
 
 ORDER = (
     (),
-    (120, 140, 150),
-    (130,),
-    (100, 180),
+    (100, 120),
+    (),
+    (110,),
     (
-        160, 170, 190, 121, 141, 110, 151, 0, 20, 131, 10, 181, 30, 40, 152, 101,
-        161, 50, 60, 142, 191, 70, 122, 11, 171, 21, 111, 182, 1, 132, 31, 41,
-        162, 102, 61, 153, 192, 143, 71, 51, 12, 22, 112, 2, 123, 172, 183, 32,
-        133, 42, 154, 144, 163, 62, 72, 103, 193, 52, 124, 13, 23, 184, 134, 113,
-        3, 173, 33, 164, 43, 155, 104, 145, 194, 63, 73, 14, 24, 53, 125, 114,
-        4, 185, 174, 135, 34, 44, 156, 146, 64, 74, 165, 54, 105, 195, 126, 15,
-        25, 115, 186, 5, 136, 175, 157, 45, 147, 35, 75, 166, 65, 196, 55, 106,
-        26, 127, 16, 116, 6, 187, 176, 137, 76, 36, 46, 66, 148, 158, 56, 27,
-        197, 167, 17, 117, 7, 128, 107, 37, 177, 138, 47, 188, 77, 67, 28, 57,
-        8, 118, 18, 168, 198, 78, 48, 38, 68, 108, 178, 58,
+        130, 150, 180, 140, 190, 101, 121, 160, 170, 20, 0, 10, 111, 40, 131, 151,
+        30, 60, 122, 141, 181, 70, 102, 191, 161, 171, 50, 11, 21, 112, 1, 41,
+        132, 152, 61, 182, 142, 71, 31, 162, 172, 192, 123, 103, 12, 51, 22, 42,
+        2, 113, 133, 62, 72, 153, 183, 32, 143, 124, 104, 163, 173, 52, 193, 13,
+        114, 23, 43, 134, 3, 154, 184, 63, 73, 144, 164, 174, 33, 125, 194, 105,
+        14, 24, 53, 44, 4, 115, 64, 74, 135, 155, 34, 185, 126, 145, 165, 175,
+        106, 54, 195, 15, 25, 116, 45, 5, 65, 75, 136, 156, 186, 127, 35, 176,
+        166, 146, 196, 55, 26, 107, 16, 6, 66, 117, 46, 76, 128, 157, 137, 167,
+        36, 197, 27, 177, 56, 108, 187, 7, 17, 67, 147, 47, 77, 118, 37, 57,
+        178, 198, 138, 158, 188, 28, 18, 168, 148, 8, 38, 58, 78, 48, 68,
     ),
 )
 
@@ -163,10 +164,12 @@
 
         def add(i, carry):
             here = pl.ds(pl.multiple_of(keep + i * block, 16), block)
-            total = self.g[here, :].astype(jnp.float32)
+            total = self.g[here, :]
+            if len(peers) > 1:
+                total = total.astype(jnp.float32)
             for peer, offset, slot, sem in peers:
                 there = pl.ds(pl.multiple_of(slot + i * block, 16), block)
-                total = total + self.inbox[there, :].astype(jnp.float32)
+                total = total + self.inbox[there, :].astype(total.dtype)
             self.g[here, :] = total.astype(jnp.bfloat16)
             return carry
 
@@ -509,7 +512,6 @@
         attend_forward(f_packed, f_mixed, f_weights, b * groups, (b + 1) * groups, False)
         result = hidden[here, :].astype(jnp.float32) + dot(f_mixed[here, :], feed_out[...])
         load_ref[b * groups : (b + 1) * groups] = result.astype(jnp.bfloat16).reshape(groups, -1, width)
-        d_mixed[here, :] = dot(adjoint[here, :], feed_out[...], NT).astype(jnp.bfloat16)
         attend_backward(f_packed, f_weights, d_mixed, d_packed, b * groups, (b + 1) * groups)
         g = dot(d_packed[here, :], feed_qkv[...], NT).astype(jnp.bfloat16).astype(jnp.float32)
         wide = hidden[here, :].astype(jnp.float32)
@@ -539,6 +541,7 @@
         there[b].start()
     for fetch in fetches:
         fetch.wait()
+    d_mixed[...] = dot(adjoint[...], feed_out[...], NT).astype(jnp.bfloat16)
     for b in range(batch):
         there[b].wait()
         feed_layer(b)

time: 115 us -> 116 us (level)
  no operation moved by 1% of the time
where the time goes in v3:
time: 116 us; the launch traced here: 115 us
  Pallas kernels  111 us (96%)
  local copies, waits for them, and re-layouts  2.81 us (2%)
  between operations  1.31 us (1%)
    pallas_call x1, Pallas kernels, on_device(): pl.pallas_call(partial(step_kernel, batch, count), out_shape=(jax.ShapeDt...  107 us
    pallas_call x1, Pallas kernels, finished(): pl.pallas_call(finish_kernel, out_shape=jax.ShapeDtypeStruct((2 * rows, s...  4.67 us

profile of v3, /device:TPU:0, one launch (start us, length us, event | category | flops | bytes accessed | tf_op | source)
XLA Modules:
  0.0 115.4 jit_solution(13169685821755803862)
XLA Ops:
  1.3 0.7 pad_bitcast_fusion
  1.9 0.7 copy.12.row_ref
  2.6 0.6 broadcast_in_dim.8.partner_ref
  3.2 106.6 %shard_map.113 = (bf16[6,128,512]{2,1,0:T(8,128)(2,1)}, bf16[6144,128]{1,0:T(8,128)(2,1)}, bf16[10240,128]{1,0:T(8,128)(2,1)}) custom-call(bf16[8,96,512]{2,1,0:T(8,128)(2,1)} %bitcast.17, s32[8,1]{1,0:T(8,128)} %copy.12.row_ref, bf16[128,512]{1,0:T(8,128)(2,1)} %table_ref.1, bf16[512,1536]{1,0:T(8,128)(2,1)} %time_qkv.1, bf16[512,512]{1,0:T(8,128)(2,1)} %time_out.1, ...), custom_call_target="tpu_custom_call" | custom-call | tf_op jit(solution)/shard_map/pallas_call | solution.py:668
  109.8 0.0 copy-start
  109.8 4.7 %shard_map.114 = f32[4096,512]{1,0:T(8,128)} custom-call(bf16[3,4,512,128]{3,2,1,0:T(8,128)(2,1)} %bitcast.15, bf16[5,4,512,128]{3,2,1,0:T(8,128)(2,1)} %bitcast.14), custom_call_target="tpu_custom_call" | custom-call | tf_op jit(solution)/shard_map/pallas_call | solution.py:611
  114.5 0.0 copy-done
  114.5 0.9 copy.15
Async XLA Ops:
  109.8 4.7 %copy-start = (bf16[6,128,512]{2,1,0:T(8,128)(2,1)S(1)}, bf16[6,128,512]{2,1,0:T(8,128)(2,1)}, u32[]{:S(2)}) copy-start(bf16[6,128,512]{2,1,0:T(8,128)(2,1)} %get-tuple-element.5) | copy-start | bytes 2359300

commit v4 on v2

--- a/solution.py
+++ b/solution.py
@@ -20,6 +20,7 @@
 STEPS = len(GROUPS)
 TURNS = 2 * STEPS + 1
 COPIES = sum(2**size - 1 for size in GROUPS)
+
 TIME_PLAN = (
     (1, (3, 2, 4, 1, 0)),
     (2, (1, 4, 0, 3, 2)),
@@ -163,10 +164,12 @@
 
         def add(i, carry):
             here = pl.ds(pl.multiple_of(keep + i * block, 16), block)
-            total = self.g[here, :].astype(jnp.float32)
+            total = self.g[here, :]
+            if len(peers) > 1:
+                total = total.astype(jnp.float32)
             for peer, offset, slot, sem in peers:
                 there = pl.ds(pl.multiple_of(slot + i * block, 16), block)
-                total = total + self.inbox[there, :].astype(jnp.float32)
+                total = total + self.inbox[there, :].astype(total.dtype)
             self.g[here, :] = total.astype(jnp.bfloat16)
             return carry
 
@@ -509,7 +512,6 @@
         attend_forward(f_packed, f_mixed, f_weights, b * groups, (b + 1) * groups, False)
         result = hidden[here, :].astype(jnp.float32) + dot(f_mixed[here, :], feed_out[...])
         load_ref[b * groups : (b + 1) * groups] = result.astype(jnp.bfloat16).reshape(groups, -1, width)
-        d_mixed[here, :] = dot(adjoint[here, :], feed_out[...], NT).astype(jnp.bfloat16)
         attend_backward(f_packed, f_weights, d_mixed, d_packed, b * groups, (b + 1) * groups)
         g = dot(d_packed[here, :], feed_qkv[...], NT).astype(jnp.bfloat16).astype(jnp.float32)
         wide = hidden[here, :].astype(jnp.float32)
@@ -539,6 +541,7 @@
         there[b].start()
     for fetch in fetches:
         fetch.wait()
+    d_mixed[...] = dot(adjoint[...], feed_out[...], NT).astype(jnp.bfloat16)
     for b in range(batch):
         there[b].wait()
         feed_layer(b)

time: 115 us -> 115 us (level)
  no operation moved by 1% of the time
where the time goes in v4:
time: 115 us
  Pallas kernels  111 us (97%)
  local copies, waits for them, and re-layouts  2.81 us (2%)
  between operations  1.31 us (1%)
    pallas_call x1, Pallas kernels, on_device(): pl.pallas_call(partial(step_kernel, batch, count), out_shape=(jax.ShapeDt...  106 us
    pallas_call x1, Pallas kernels, finished(): pl.pallas_call(finish_kernel, out_shape=jax.ShapeDtypeStruct((2 * rows, s...  4.67 us

profile of v4, /device:TPU:0, one launch (start us, length us, event | category | flops | bytes accessed | tf_op | source)
XLA Modules:
  0.0 114.6 jit_solution(808120682791198466)
XLA Ops:
  1.3 0.7 pad_bitcast_fusion
  1.9 0.7 copy.12.row_ref
  2.6 0.6 broadcast_in_dim.8.partner_ref
  3.2 105.9 %shard_map.113 = (bf16[6,128,512]{2,1,0:T(8,128)(2,1)}, bf16[6144,128]{1,0:T(8,128)(2,1)}, bf16[10240,128]{1,0:T(8,128)(2,1)}) custom-call(bf16[8,96,512]{2,1,0:T(8,128)(2,1)} %bitcast.17, s32[8,1]{1,0:T(8,128)} %copy.12.row_ref, bf16[128,512]{1,0:T(8,128)(2,1)} %table_ref.1, bf16[512,1536]{1,0:T(8,128)(2,1)} %time_qkv.1, bf16[512,512]{1,0:T(8,128)(2,1)} %time_out.1, ...), custom_call_target="tpu_custom_call" | custom-call | tf_op jit(solution)/shard_map/pallas_call | solution.py:668
  109.1 0.0 copy-start
  109.1 4.7 %shard_map.114 = f32[4096,512]{1,0:T(8,128)} custom-call(bf16[3,4,512,128]{3,2,1,0:T(8,128)(2,1)} %bitcast.15, bf16[5,4,512,128]{3,2,1,0:T(8,128)(2,1)} %bitcast.14), custom_call_target="tpu_custom_call" | custom-call | tf_op jit(solution)/shard_map/pallas_call | solution.py:611
  113.8 0.0 copy-done
  113.8 0.9 copy.15
Async XLA Ops:
  109.1 4.7 %copy-start = (bf16[6,128,512]{2,1,0:T(8,128)(2,1)S(1)}, bf16[6,128,512]{2,1,0:T(8,128)(2,1)}, u32[]{:S(2)}) copy-start(bf16[6,128,512]{2,1,0:T(8,128)(2,1)} %get-tuple-element.5) | copy-start | bytes 2359300

commit v5 on v4

--- a/solution.py
+++ b/solution.py
@@ -229,7 +229,7 @@
         following = []
         if stage < STEPS:
             for copy in self.rs_copies(j, stage):
-                copy.wait()
+                copy.wait_recv()
             self.rs_add(j, stage)
             if stage + 1 < STEPS:
                 following = self.rs_copies(j, stage + 1)
@@ -237,19 +237,24 @@
                 following = [self.pair_copy(j, n) for n in range(len(PAIRS))]
         elif stage == STEPS:
             for n in range(len(PAIRS)):
-                self.pair_copy(j, n).wait()
+                self.pair_copy(j, n).wait_recv()
             self.pair_mean(j)
             following = self.ag_copies(j, STEPS - 1)
         else:
             s = 2 * STEPS - stage
             for copy in self.ag_copies(j, s):
-                copy.wait()
+                copy.wait_recv()
             following = self.ag_copies(j, s - 1) if s > 0 else [self.out_copy(j)]
         for copy in following:
             copy.start()
 
     def finish(self):
         for j in range(len(self.chains)):
+            sent = [self.pair_copy(j, n) for n in range(len(PAIRS))]
+            for s in range(STEPS):
+                sent += self.rs_copies(j, s) + self.ag_copies(j, s)
+            for copy in sent:
+                copy.wait_send()
             self.out_copy(j).wait()
 
 

time: 115 us -> 115 us (level)
  no operation moved by 1% of the time
where the time goes in v5:
time: 115 us
  Pallas kernels  111 us (97%)
  local copies, waits for them, and re-layouts  2.81 us (2%)
  between operations  1.31 us (1%)
    pallas_call x1, Pallas kernels, on_device(): pl.pallas_call(partial(step_kernel, batch, count), out_shape=(jax.ShapeDt...  106 us
    pallas_call x1, Pallas kernels, finished(): pl.pallas_call(finish_kernel, out_shape=jax.ShapeDtypeStruct((2 * rows, s...  4.67 us

profile of v5, /device:TPU:0, one launch (start us, length us, event | category | flops | bytes accessed | tf_op | source)
XLA Modules:
  0.0 114.8 jit_solution(16696746121618179178)
XLA Ops:
  1.3 0.7 pad_bitcast_fusion
  1.9 0.7 copy.12.row_ref
  2.6 0.6 broadcast_in_dim.8.partner_ref
  3.2 106.0 %shard_map.113 = (bf16[6,128,512]{2,1,0:T(8,128)(2,1)}, bf16[6144,128]{1,0:T(8,128)(2,1)}, bf16[10240,128]{1,0:T(8,128)(2,1)}) custom-call(bf16[8,96,512]{2,1,0:T(8,128)(2,1)} %bitcast.17, s32[8,1]{1,0:T(8,128)} %copy.12.row_ref, bf16[128,512]{1,0:T(8,128)(2,1)} %table_ref.1, bf16[512,1536]{1,0:T(8,128)(2,1)} %time_qkv.1, bf16[512,512]{1,0:T(8,128)(2,1)} %time_out.1, ...), custom_call_target="tpu_custom_call" | custom-call | tf_op jit(solution)/shard_map/pallas_call | solution.py:673
  109.2 0.0 copy-start
  109.2 4.7 %shard_map.114 = f32[4096,512]{1,0:T(8,128)} custom-call(bf16[3,4,512,128]{3,2,1,0:T(8,128)(2,1)} %bitcast.15, bf16[5,4,512,128]{3,2,1,0:T(8,128)(2,1)} %bitcast.14), custom_call_target="tpu_custom_call" | custom-call | tf_op jit(solution)/shard_map/pallas_call | solution.py:616
  113.9 0.0 copy-done
  113.9 0.9 copy.15
Async XLA Ops:
  109.2 4.7 %copy-start = (bf16[6,128,512]{2,1,0:T(8,128)(2,1)S(1)}, bf16[6,128,512]{2,1,0:T(8,128)(2,1)}, u32[]{:S(2)}) copy-start(bf16[6,128,512]{2,1,0:T(8,128)(2,1)} %get-tuple-element.5) | copy-start | bytes 2359300
